TPU v7x, 512 devices: a whole 4x8x8 slice. The times are simulated.
512 devices in a mesh: tm: 128 (over y, z, core), rows: 4 (over x).
Axes of the slice: x: 4, y: 8, z: 8, core: 2. Of those that a mesh axis runs over, the one named last changes fastest.
Arguments:
- source_term: float32 [128, 128, 1024], P('tm', 'rows'), may hold values from -6 to 6
- iterate: float32 [128, 128, 1024], P('tm', 'rows'), may hold values from -6 to 6
- initial: float32 [128, 1024], P('rows'), may hold values from -6 to 6
- conductivity: float32 [128, 1024], P('rows'), may hold values from 0.25 to 2
Outputs:
- correction: float32 [128, 128, 1024], P('tm', 'rows')
All inputs are finite; a program needn't handle non-finite values.
Results may differ from a plain program's by a relative error of at most 0.0003.
Values sent between devices are 32-bit elements; how exact they have to be, the bound alone decides.
A program may use at most 64 MiB of HBM per device.

v0:
```python
import math

import jax
import jax.numpy as jnp
from jax import lax
from jax.sharding import PartitionSpec as P

SWEEPS = 6


time_step = 0.5
wrap_factor = 0.25
chebyshev_spread = 0.7


def shifted(value, axis, by):
    peers = lax.axis_size(axis)
    pairs = [(i, i + by) for i in range(peers) if 0 <= i + by < peers]
    return lax.ppermute(value, axis, pairs)


def extended(value, sides, width):
    for axis, dim in sides:
        peers, length = (lax.axis_size(axis), value.shape[dim])
        up = [(i, (i + 1) % peers) for i in range(peers - 1)]
        down = [(j, i) for i, j in up]
        last = lax.slice_in_dim(value, length - width, length, axis=dim)
        first = lax.slice_in_dim(value, 0, width, axis=dim)
        before = lax.ppermute(last, axis, up)
        after = lax.ppermute(first, axis, down)
        value = jnp.concatenate([before, value, after], axis=dim)
    return value


def sweep_weights(count):
    return [
        1.0 / (1.0 + chebyshev_spread * math.cos(math.pi * (2 * sweep + 1) / (2 * count)))
        for sweep in range(count)
    ]


def build_tables(window):
    freq_index = jnp.arange(window, dtype=jnp.int32)
    products = freq_index[:, None] * freq_index[None, :] % window
    angles = products.astype(jnp.float32) * (2.0 * math.pi / window)
    cosine = jnp.cos(angles)
    sine = jnp.sin(angles)
    middle = window // 2
    keep_real = (freq_index <= middle).astype(jnp.float32)
    keep_imag = ((freq_index >= 1) & (freq_index < middle)).astype(jnp.float32)
    weighting = jnp.exp(freq_index.astype(jnp.float32) * (math.log(wrap_factor) / window))
    forward = jnp.stack(
        [
            cosine * keep_real[:, None] * weighting[None, :],
            -sine * keep_imag[:, None] * weighting[None, :],
        ]
    )
    multiplicity = keep_real * (1.0 + keep_imag)
    scale_back = 1.0 / (window * weighting)
    inverse = (
        jnp.stack([cosine.T * multiplicity[None, :], -sine.T * (2.0 * keep_imag)[None, :]], axis=1)
        * scale_back[:, None, None]
    )
    root_factor = math.exp(math.log(wrap_factor) / window)
    base_angles = freq_index.astype(jnp.float32) * (2.0 * math.pi / window)
    shift_real = 1.0 - root_factor * jnp.cos(base_angles)
    shift_coupling = root_factor * jnp.sin(base_angles) * keep_imag
    return (forward, inverse, shift_real, shift_coupling)


def stencil(field, row_padded, left_column, right_column):
    widened = jnp.concatenate([left_column, field, right_column], axis=-1)
    return (
        4.0 * field
        - row_padded[..., :-2, :]
        - row_padded[..., 2:, :]
        - widened[..., :-2]
        - widened[..., 2:]
    )


def relax(source_pair, shift_one, shift_two, coupling, conductivity, neighbours):
    diffusion = time_step * conductivity
    diag_one = shift_one + 4.0 * diffusion
    diag_two = shift_two + 4.0 * diffusion
    determinant = diag_one * diag_two + coupling * coupling
    field = jnp.zeros_like(source_pair)
    for sweep, weight in enumerate(sweep_weights(SWEEPS)):
        if sweep == 0:
            defect_real = source_pair[0]
            defect_imag = source_pair[1]
        else:
            coupled = diffusion[None] * neighbours(field)
            defect_real = source_pair[0] - (shift_one * field[0] + coupled[0] - coupling * field[1])
            defect_imag = source_pair[1] - (shift_two * field[1] + coupled[1] + coupling * field[0])
        change = jnp.stack(
            [
                (diag_two * defect_real + coupling * defect_imag) / determinant,
                (diag_one * defect_imag - coupling * defect_real) / determinant,
            ]
        )
        field = field + weight * change
    return field


def shards(source_term, iterate, initial, conductivity):
    window = lax.axis_size("tm")
    position = lax.axis_index("tm")
    row_count, columns = conductivity.shape
    half_block = row_count * columns // (2 * window)
    forward, inverse, shift_real, shift_coupling = build_tables(window)
    previous = shifted(iterate, "tm", 1)
    previous = previous + jnp.where(position == 0, 1.0, 0.0) * initial[None]
    row_padded = extended(iterate, (("rows", 1),), 1)
    zero_column = jnp.zeros((1, row_count, 1), jnp.float32)
    operated = conductivity[None] * stencil(iterate, row_padded, zero_column, zero_column)
    residual = source_term - (iterate + time_step * operated - previous)
    points = lax.all_to_all(
        residual.reshape(2, window, half_block), "tm", split_axis=1, concat_axis=1, tiled=True
    )
    spectrum = jnp.einsum("ckn,hnb->ckhb", forward, points, precision=lax.Precision.HIGHEST)
    slab = lax.all_to_all(spectrum, "tm", split_axis=1, concat_axis=3, tiled=True).reshape(
        2, row_count, columns
    )
    shift_one = shift_real[position]
    coupling = shift_coupling[position]
    side_zero = jnp.zeros((2, row_count, 1), jnp.float32)

    def neighbours(field):
        padded = extended(field, (("rows", 1),), 1)
        return stencil(field, padded, side_zero, side_zero)

    solved = relax(slab, shift_one, shift_one, coupling, conductivity, neighbours)
    gathered = lax.all_to_all(
        solved.reshape(2, 1, 2, window, half_block), "tm", split_axis=3, concat_axis=1, tiled=True
    )
    gathered = gathered.reshape(2, window, 2, half_block)
    grid_points = jnp.einsum("nck,ckhb->nhb", inverse, gathered, precision=lax.Precision.HIGHEST)
    returned = lax.all_to_all(grid_points, "tm", split_axis=0, concat_axis=2, tiled=True)
    return returned.reshape(1, row_count, columns)


def solution(mesh):
    in_specs = (P("tm", "rows", None), P("tm", "rows", None), P("rows", None), P("rows", None))
    out_specs = P("tm", "rows", None)
    return jax.shard_map(shards, mesh=mesh, in_specs=in_specs, out_specs=out_specs, check_vma=False)
```

profile of v0, /device:TPU:1, one launch (start us, length us, event | category | flops | bytes accessed | tf_op | source)
XLA Modules:
  0.0 168.2 jit_solution(9129085285793937894)
XLA Ops:
  0.0 5.4 %collective-permute-start.2 = (f32[1,32,1024]{2,1,0:T(8,128)}, f32[1,32,1024]{2,1,0:T(8,128)S(1)}, u32[]{:S(2)}, u32[]{:S(2)}) collective-permute-start(f32[1,32,1024]{2,1,0:T(8,128)} %param.5), channel_id=1, source_target_pairs={{0,4},{4,8},{8,12},{12,16},{16,20},{20,24},{24,28},{28,32},{32,36}... | collective-permute-start | bytes 393224 | tf_op jit(solution)/shard_map/ppermute | solution.py:19
  6.2 3.1 %collective-permute-start = (f32[1,1,1024]{2,1,0:T(1,128)S(1)}, f32[1,1,1024]{2,1,0:T(1,128)S(1)}, u32[]{:S(2)}, u32[]{:S(2)}) collective-permute-start(f32[1,1,1024]{2,1,0:T(1,128)S(1)} %get-tuple-element.35), channel_id=1, source_target_pairs={{0,1},{1,2},{2,3},{4,5},{5,6},{6,7},{8,9},{9,10},{10,11},{12,13},{... | collective-permute-start | bytes 12296 | tf_op jit(solution)/shard_map/ppermute | solution.py:29
  10.6 3.0 %collective-permute-done.1 = f32[1,1,1024]{2,1,0:T(1,128)S(1)} collective-permute-done((f32[1,1,1024]{2,1,0:T(1,128)S(1)}, f32[1,1,1024]{2,1,0:T(1,128)S(1)}, u32[]{:S(2)}, u32[]{:S(2)}) %collective-permute-start.1) | collective-permute-done | bytes 4128 | tf_op jit(solution)/shard_map/ppermute | solution.py:30
  13.7 1.4 fusion.43
  15.9 16.4 %all-to-all-start = ((f32[2,128,128]{2,0,1:T(2,128)}), f32[2,128,128]{2,0,1:T(2,128)S(1)}, u32[]{:S(2)}, u32[]{:S(2)}) async-start(f32[2,128,128]{2,0,1:T(2,128)} %copy.9), calls=%async_computation | async-start | bytes 262144 | tf_op jit(solution)/shard_map/all_to_all | solution.py:118
  32.5 12.0 %all-to-all-done = f32[2,128,128]{2,0,1:T(2,128)S(1)} async-done(((f32[2,128,128]{2,0,1:T(2,128)}), f32[2,128,128]{2,0,1:T(2,128)S(1)}, u32[]{:S(2)}, u32[]{:S(2)}) %all-to-all-start) | async-done | bytes 131104 | tf_op jit(solution)/shard_map/all_to_all | solution.py:118
  45.8 6.1 %all-to-all-start.1 = ((f32[2,128,2,128]{3,2,0,1:T(2,128)}), f32[2,128,2,128]{3,2,0,1:T(2,128)S(1)}, u32[]{:S(2)}, u32[]{:S(2)}) async-start(f32[2,128,2,128]{3,2,0,1:T(2,128)} %copy.11), calls=%async_computation.1 | async-start | bytes 524288 | tf_op jit(solution)/shard_map/all_to_all | solution.py:122
  54.5 11.7 %all-to-all-done.1 = f32[2,128,2,128]{3,2,0,1:T(2,128)S(1)} async-done(((f32[2,128,2,128]{3,2,0,1:T(2,128)}), f32[2,128,2,128]{3,2,0,1:T(2,128)S(1)}, u32[]{:S(2)}, u32[]{:S(2)}) %all-to-all-start.1) | async-done | bytes 262176 | tf_op jit(solution)/shard_map/all_to_all | solution.py:122
  68.7 3.1 %collective-permute-start.3 = (f32[2,1,1024]{2,1,0:T(1,128)S(1)}, f32[2,1,1024]{2,1,0:T(1,128)S(1)}, u32[]{:S(2)}, u32[]{:S(2)}) collective-permute-start(f32[2,1,1024]{2,1,0:T(1,128)S(1)} %get-tuple-element.30), channel_id=1, source_target_pairs={{0,1},{1,2},{2,3},{4,5},{5,6},{6,7},{8,9},{9,10},{10,11},{12,13},{... | collective-permute-start | bytes 24584 | tf_op jit(solution)/shard_map/ppermute | solution.py:29
  73.2 3.1 %collective-permute-done.4 = f32[2,1,1024]{2,1,0:T(1,128)S(1)} collective-permute-done((f32[2,1,1024]{2,1,0:T(1,128)S(1)}, f32[2,1,1024]{2,1,0:T(1,128)S(1)}, u32[]{:S(2)}, u32[]{:S(2)}) %collective-permute-start.4) | collective-permute-done | bytes 8224 | tf_op jit(solution)/shard_map/ppermute | solution.py:30
  76.5 1.4 add_divide_fusion.4
  79.2 2.8 %collective-permute-start.5 = (f32[2,1,1024]{2,1,0:T(1,128)S(1)}, f32[2,1,1024]{2,1,0:T(1,128)S(1)}, u32[]{:S(2)}, u32[]{:S(2)}) collective-permute-start(f32[2,1,1024]{2,1,0:T(1,128)S(1)} %get-tuple-element.28), channel_id=1, source_target_pairs={{0,1},{1,2},{2,3},{4,5},{5,6},{6,7},{8,9},{9,10},{10,11},{12,13},{... | collective-permute-start | bytes 24584 | tf_op jit(solution)/shard_map/ppermute | solution.py:29
  83.4 3.1 %collective-permute-done.6 = f32[2,1,1024]{2,1,0:T(1,128)S(1)} collective-permute-done((f32[2,1,1024]{2,1,0:T(1,128)S(1)}, f32[2,1,1024]{2,1,0:T(1,128)S(1)}, u32[]{:S(2)}, u32[]{:S(2)}) %collective-permute-start.6) | collective-permute-done | bytes 8224 | tf_op jit(solution)/shard_map/ppermute | solution.py:30
  86.7 1.4 add_divide_fusion.3
  89.5 1.9 %collective-permute-start.7 = (f32[2,1,1024]{2,1,0:T(1,128)S(1)}, f32[2,1,1024]{2,1,0:T(1,128)S(1)}, u32[]{:S(2)}, u32[]{:S(2)}) collective-permute-start(f32[2,1,1024]{2,1,0:T(1,128)S(1)} %get-tuple-element.26), channel_id=1, source_target_pairs={{0,1},{1,2},{2,3},{4,5},{5,6},{6,7},{8,9},{9,10},{10,11},{12,13},{... | collective-permute-start | bytes 24584 | tf_op jit(solution)/shard_map/ppermute | solution.py:29
  92.7 3.1 %collective-permute-done.8 = f32[2,1,1024]{2,1,0:T(1,128)S(1)} collective-permute-done((f32[2,1,1024]{2,1,0:T(1,128)S(1)}, f32[2,1,1024]{2,1,0:T(1,128)S(1)}, u32[]{:S(2)}, u32[]{:S(2)}) %collective-permute-start.8) | collective-permute-done | bytes 8224 | tf_op jit(solution)/shard_map/ppermute | solution.py:30
  100.2 4.0 %collective-permute-start.9 = (f32[2,1,1024]{2,1,0:T(1,128)S(1)}, f32[2,1,1024]{2,1,0:T(1,128)S(1)}, u32[]{:S(2)}, u32[]{:S(2)}) collective-permute-start(f32[2,1,1024]{2,1,0:T(1,128)S(1)} %get-tuple-element.24), channel_id=1, source_target_pairs={{0,1},{1,2},{2,3},{4,5},{5,6},{6,7},{8,9},{9,10},{10,11},{12,13},{... | collective-permute-start | bytes 24584 | tf_op jit(solution)/shard_map/ppermute | solution.py:29
  105.2 1.4 add_divide_fusion.1
  108.0 3.6 %collective-permute-start.11 = (f32[2,1,1024]{2,1,0:T(1,128)S(1)}, f32[2,1,1024]{2,1,0:T(1,128)S(1)}, u32[]{:S(2)}, u32[]{:S(2)}) collective-permute-start(f32[2,1,1024]{2,1,0:T(1,128)S(1)} %get-tuple-element.22), channel_id=1, source_target_pairs={{0,1},{1,2},{2,3},{4,5},{5,6},{6,7},{8,9},{9,10},{10,11},{12,13},{... | collective-permute-start | bytes 24584 | tf_op jit(solution)/shard_map/ppermute | solution.py:29
  113.3 2.7 %collective-permute-done.12 = f32[2,1,1024]{2,1,0:T(1,128)S(1)} collective-permute-done((f32[2,1,1024]{2,1,0:T(1,128)S(1)}, f32[2,1,1024]{2,1,0:T(1,128)S(1)}, u32[]{:S(2)}, u32[]{:S(2)}) %collective-permute-start.12) | collective-permute-done | bytes 8224 | tf_op jit(solution)/shard_map/ppermute | solution.py:30
  116.2 1.4 add_divide_fusion
  120.0 13.8 %all-to-all-start.2 = ((f32[2,1,2,128,128]{4,0,2,1,3:T(2,128)}), f32[2,1,2,128,128]{4,0,2,1,3:T(2,128)S(1)}, u32[]{:S(2)}, u32[]{:S(2)}) async-start(f32[2,1,2,128,128]{4,0,2,1,3:T(2,128)} %copy.14), calls=%async_computation.2 | async-start | bytes 524288 | tf_op jit(solution)/shard_map/all_to_all | solution.py:134
  134.2 14.0 %all-to-all-done.2 = f32[2,1,2,128,128]{4,0,2,1,3:T(2,128)S(1)} async-done(((f32[2,1,2,128,128]{4,0,2,1,3:T(2,128)}), f32[2,1,2,128,128]{4,0,2,1,3:T(2,128)S(1)}, u32[]{:S(2)}, u32[]{:S(2)}) %all-to-all-start.2) | async-done | bytes 262176 | tf_op jit(solution)/shard_map/all_to_all | solution.py:134
  148.6 18.9 %all_to_all.50 = f32[128,2,128]{2,1,0:T(2,128)S(1)} all-to-all(f32[128,2,128]{2,1,0:T(2,128)S(1)} %copy.16), channel_id=1, replica_groups=mesh['tm'=128,'rows'=4] {'tm'}, dimensions={0} | all-to-all | bytes 262144 | tf_op jit(solution)/shard_map/all_to_all | solution.py:139
  (77 shorter events, 27.6 us)
Async XLA Ops:
  0.0 13.7 %collective-permute-start.2 = (f32[1,32,1024]{2,1,0:T(8,128)}, f32[1,32,1024]{2,1,0:T(8,128)S(1)}, u32[]{:S(2)}, u32[]{:S(2)}) collective-permute-start(f32[1,32,1024]{2,1,0:T(8,128)} %param.5), channel_id=1, source_target_pairs={{0,4},{4,8},{8,12},{12,16},{16,20},{20,24},{24,28},{28,32},{32,36}... | collective-permute-start | bytes 393224 | tf_op jit(solution)/shard_map/ppermute | solution.py:19
  6.2 4.4 %collective-permute-start = (f32[1,1,1024]{2,1,0:T(1,128)S(1)}, f32[1,1,1024]{2,1,0:T(1,128)S(1)}, u32[]{:S(2)}, u32[]{:S(2)}) collective-permute-start(f32[1,1,1024]{2,1,0:T(1,128)S(1)} %get-tuple-element.35), channel_id=1, source_target_pairs={{0,1},{1,2},{2,3},{4,5},{5,6},{6,7},{8,9},{9,10},{10,11},{12,13},{... | collective-permute-start | bytes 12296 | tf_op jit(solution)/shard_map/ppermute | solution.py:29
  9.3 4.4 %collective-permute-start.1 = (f32[1,1,1024]{2,1,0:T(1,128)S(1)}, f32[1,1,1024]{2,1,0:T(1,128)S(1)}, u32[]{:S(2)}, u32[]{:S(2)}) collective-permute-start(f32[1,1,1024]{2,1,0:T(1,128)S(1)} %get-tuple-element.36), channel_id=1, source_target_pairs={{1,0},{2,1},{3,2},{5,4},{6,5},{7,6},{9,8},{10,9},{11,10},{13,12},{... | collective-permute-start | bytes 12296 | tf_op jit(solution)/shard_map/ppermute | solution.py:30
  15.9 28.6 %all-to-all-start = ((f32[2,128,128]{2,0,1:T(2,128)}), f32[2,128,128]{2,0,1:T(2,128)S(1)}, u32[]{:S(2)}, u32[]{:S(2)}) async-start(f32[2,128,128]{2,0,1:T(2,128)} %copy.9), calls=%async_computation | async-start | bytes 262144 | tf_op jit(solution)/shard_map/all_to_all | solution.py:118
  45.8 20.5 %all-to-all-start.1 = ((f32[2,128,2,128]{3,2,0,1:T(2,128)}), f32[2,128,2,128]{3,2,0,1:T(2,128)S(1)}, u32[]{:S(2)}, u32[]{:S(2)}) async-start(f32[2,128,2,128]{3,2,0,1:T(2,128)} %copy.11), calls=%async_computation.1 | async-start | bytes 524288 | tf_op jit(solution)/shard_map/all_to_all | solution.py:122
  66.4 0.9 copy-start
  68.7 4.4 %collective-permute-start.3 = (f32[2,1,1024]{2,1,0:T(1,128)S(1)}, f32[2,1,1024]{2,1,0:T(1,128)S(1)}, u32[]{:S(2)}, u32[]{:S(2)}) collective-permute-start(f32[2,1,1024]{2,1,0:T(1,128)S(1)} %get-tuple-element.30), channel_id=1, source_target_pairs={{0,1},{1,2},{2,3},{4,5},{5,6},{6,7},{8,9},{9,10},{10,11},{12,13},{... | collective-permute-start | bytes 24584 | tf_op jit(solution)/shard_map/ppermute | solution.py:29
  71.8 4.4 %collective-permute-start.4 = (f32[2,1,1024]{2,1,0:T(1,128)S(1)}, f32[2,1,1024]{2,1,0:T(1,128)S(1)}, u32[]{:S(2)}, u32[]{:S(2)}) collective-permute-start(f32[2,1,1024]{2,1,0:T(1,128)S(1)} %get-tuple-element.31), channel_id=1, source_target_pairs={{1,0},{2,1},{3,2},{5,4},{6,5},{7,6},{9,8},{10,9},{11,10},{13,12},{... | collective-permute-start | bytes 24584 | tf_op jit(solution)/shard_map/ppermute | solution.py:30
  79.2 4.1 %collective-permute-start.5 = (f32[2,1,1024]{2,1,0:T(1,128)S(1)}, f32[2,1,1024]{2,1,0:T(1,128)S(1)}, u32[]{:S(2)}, u32[]{:S(2)}) collective-permute-start(f32[2,1,1024]{2,1,0:T(1,128)S(1)} %get-tuple-element.28), channel_id=1, source_target_pairs={{0,1},{1,2},{2,3},{4,5},{5,6},{6,7},{8,9},{9,10},{10,11},{12,13},{... | collective-permute-start | bytes 24584 | tf_op jit(solution)/shard_map/ppermute | solution.py:29
  82.1 4.4 %collective-permute-start.6 = (f32[2,1,1024]{2,1,0:T(1,128)S(1)}, f32[2,1,1024]{2,1,0:T(1,128)S(1)}, u32[]{:S(2)}, u32[]{:S(2)}) collective-permute-start(f32[2,1,1024]{2,1,0:T(1,128)S(1)} %get-tuple-element.29), channel_id=1, source_target_pairs={{1,0},{2,1},{3,2},{5,4},{6,5},{7,6},{9,8},{10,9},{11,10},{13,12},{... | collective-permute-start | bytes 24584 | tf_op jit(solution)/shard_map/ppermute | solution.py:30
  89.5 3.2 %collective-permute-start.7 = (f32[2,1,1024]{2,1,0:T(1,128)S(1)}, f32[2,1,1024]{2,1,0:T(1,128)S(1)}, u32[]{:S(2)}, u32[]{:S(2)}) collective-permute-start(f32[2,1,1024]{2,1,0:T(1,128)S(1)} %get-tuple-element.26), channel_id=1, source_target_pairs={{0,1},{1,2},{2,3},{4,5},{5,6},{6,7},{8,9},{9,10},{10,11},{12,13},{... | collective-permute-start | bytes 24584 | tf_op jit(solution)/shard_map/ppermute | solution.py:29
  91.4 4.4 %collective-permute-start.8 = (f32[2,1,1024]{2,1,0:T(1,128)S(1)}, f32[2,1,1024]{2,1,0:T(1,128)S(1)}, u32[]{:S(2)}, u32[]{:S(2)}) collective-permute-start(f32[2,1,1024]{2,1,0:T(1,128)S(1)} %get-tuple-element.27), channel_id=1, source_target_pairs={{1,0},{2,1},{3,2},{5,4},{6,5},{7,6},{9,8},{10,9},{11,10},{13,12},{... | collective-permute-start | bytes 24584 | tf_op jit(solution)/shard_map/ppermute | solution.py:30
  98.9 5.3 %collective-permute-start.10 = (f32[2,1,1024]{2,1,0:T(1,128)S(1)}, f32[2,1,1024]{2,1,0:T(1,128)S(1)}, u32[]{:S(2)}, u32[]{:S(2)}) collective-permute-start(f32[2,1,1024]{2,1,0:T(1,128)S(1)} %get-tuple-element.25), channel_id=1, source_target_pairs={{1,0},{2,1},{3,2},{5,4},{6,5},{7,6},{9,8},{10,9},{11,10},{13,12},{... | collective-permute-start | bytes 24584 | tf_op jit(solution)/shard_map/ppermute | solution.py:30
  100.2 4.8 %collective-permute-start.9 = (f32[2,1,1024]{2,1,0:T(1,128)S(1)}, f32[2,1,1024]{2,1,0:T(1,128)S(1)}, u32[]{:S(2)}, u32[]{:S(2)}) collective-permute-start(f32[2,1,1024]{2,1,0:T(1,128)S(1)} %get-tuple-element.24), channel_id=1, source_target_pairs={{0,1},{1,2},{2,3},{4,5},{5,6},{6,7},{8,9},{9,10},{10,11},{12,13},{... | collective-permute-start | bytes 24584 | tf_op jit(solution)/shard_map/ppermute | solution.py:29
  108.0 5.3 %collective-permute-start.11 = (f32[2,1,1024]{2,1,0:T(1,128)S(1)}, f32[2,1,1024]{2,1,0:T(1,128)S(1)}, u32[]{:S(2)}, u32[]{:S(2)}) collective-permute-start(f32[2,1,1024]{2,1,0:T(1,128)S(1)} %get-tuple-element.22), channel_id=1, source_target_pairs={{0,1},{1,2},{2,3},{4,5},{5,6},{6,7},{8,9},{9,10},{10,11},{12,13},{... | collective-permute-start | bytes 24584 | tf_op jit(solution)/shard_map/ppermute | solution.py:29
  111.6 4.4 %collective-permute-start.12 = (f32[2,1,1024]{2,1,0:T(1,128)S(1)}, f32[2,1,1024]{2,1,0:T(1,128)S(1)}, u32[]{:S(2)}, u32[]{:S(2)}) collective-permute-start(f32[2,1,1024]{2,1,0:T(1,128)S(1)} %get-tuple-element.23), channel_id=1, source_target_pairs={{1,0},{2,1},{3,2},{5,4},{6,5},{7,6},{9,8},{10,9},{11,10},{13,12},{... | collective-permute-start | bytes 24584 | tf_op jit(solution)/shard_map/ppermute | solution.py:30
  120.0 28.1 %all-to-all-start.2 = ((f32[2,1,2,128,128]{4,0,2,1,3:T(2,128)}), f32[2,1,2,128,128]{4,0,2,1,3:T(2,128)S(1)}, u32[]{:S(2)}, u32[]{:S(2)}) async-start(f32[2,1,2,128,128]{4,0,2,1,3:T(2,128)} %copy.14), calls=%async_computation.2 | async-start | bytes 524288 | tf_op jit(solution)/shard_map/all_to_all | solution.py:134
where the time goes:
time: 169 us; the launch traced here: 168 us
  starting transfers between devices  68 us (40%)
  waiting for transfers between devices  53.5 us (32%)
  blocking collectives  18.9 us (11%)
  other arithmetic  18.5 us (11%)
  local copies, waits for them, and re-layouts  6.82 us (4%)
  between operations  1.86 us (1%)
    all_to_all x1, blocking collectives, shards(): lax.all_to_all(grid_points, 'tm', split_axis=0, concat_axis=2, tiled=True)  18.9 us
    ppermute x6, starting transfers between devices, extended(): before = lax.ppermute(last, axis, up)  18.6 us
    all_to_all x1, starting transfers between devices, shards(): lax.all_to_all(residual.reshape(2, window, half_block), 'tm', split_axis=...  16.4 us
    ppermute x6, waiting for transfers between devices, extended(): after = lax.ppermute(first, axis, down)  15 us
    all_to_all x1, waiting for transfers between devices, shards(): lax.all_to_all(solved.reshape(2, 1, 2, window, half_block), 'tm', split_a...  14 us
    all_to_all x1, starting transfers between devices, shards(): lax.all_to_all(solved.reshape(2, 1, 2, window, half_block), 'tm', split_a...  13.8 us
    all_to_all x1, waiting for transfers between devices, shards(): lax.all_to_all(residual.reshape(2, window, half_block), 'tm', split_axis=...  12 us
    all_to_all x1, waiting for transfers between devices, shards(): lax.all_to_all(spectrum, 'tm', split_axis=1, concat_axis=3, tiled=True)  11.7 us
  transfers between devices with their start and end apart: 16, of which 9 were waited for; matrix products, arithmetic and copies ran while one was open for 2% of the time, Pallas kernels for 0%

commit v1 on v0

v1 whole, which is shorter than its diff:
```python
import functools
import math

import jax
import jax.numpy as jnp
import numpy as np
from jax import lax
from jax.experimental import pallas as pl
from jax.experimental.pallas import tpu as pltpu
from jax.sharding import PartitionSpec as P

MESH = pl.DeviceIdType.MESH

SWEEPS = 6
time_step = 0.5
wrap_factor = 0.25
chebyshev_spread = 0.7

STEPS = 128
COLS = 1024
ROWS = 32
TILE = 8
HALO = SWEEPS - 1
SPAN = TILE + 2 * HALO
GROUPS = 7
DEPTH = 6
TOP = 8 - HALO
FRAME = ROWS + 16


def sweep_weights(count):
    return [
        1.0 / (1.0 + chebyshev_spread * math.cos(math.pi * (2 * sweep + 1) / (2 * count)))
        for sweep in range(count)
    ]


def tables():
    half = STEPS // 2
    k = np.arange(half)
    n = np.arange(STEPS)
    angle = 2.0 * np.pi * (k[:, None] * n[None, :] % STEPS) / STEPS
    weight = wrap_factor ** (n / STEPS)
    cosine, sine = np.cos(angle), np.sin(angle)
    alternating = np.where(n % 2 == 0, 1.0, -1.0)
    forward = np.concatenate([cosine, -sine]) * weight
    forward[half] = alternating * weight
    multiplicity = np.where(k == 0, 1.0, 2.0)[:, None]
    inverse = np.concatenate([cosine * multiplicity, -2.0 * sine])
    inverse[half] = alternating
    inverse = (inverse / (STEPS * weight)).T
    beta = wrap_factor ** (1.0 / STEPS)
    theta = 2.0 * np.pi * k / STEPS
    shift_one = 1.0 - beta * np.cos(theta)
    shift_two = shift_one.copy()
    shift_two[0] = 1.0 + beta
    coupling = beta * np.sin(theta)
    coupling[0] = 0.0
    wide = [np.repeat(v[:, None], 128, axis=1) for v in (shift_one, shift_two, coupling)]
    shifts = np.concatenate(wide).astype(np.float32)

    def parts(matrix):
        whole = matrix.astype(np.float32)
        high = whole.astype(jnp.bfloat16)
        low = (whole - high.astype(np.float32)).astype(jnp.bfloat16)
        return [high, low]

    select = np.zeros((DEPTH * 128, 256), np.float32)
    for row in range(ROWS):
        g, s = divmod(row + HALO, DEPTH)
        for c in range(TILE):
            select[128 * s + SPAN * g + HALO + c, 128 * (row // 16) + 8 * (row % 16) + c] = 1.0
    matrices = np.concatenate(parts(forward) + parts(inverse))
    return shifts, matrices, select.astype(jnp.bfloat16)


def residual_pack_send(me, y, row_slab, it, src, prv, cnd, res, out, inc, sems, local_sem):
    lane = lax.broadcasted_iota(jnp.int32, (8, 128), 1)
    column = lax.broadcasted_iota(jnp.int32, (FRAME, COLS), 1)
    field = it[...]
    left = jnp.where(column == 0, 0.0, pltpu.roll(field, 1, 1))
    right = jnp.where(column == COLS - 1, 0.0, pltpu.roll(field, COLS - 1, 1))
    lap = 4.0 * field - pltpu.roll(field, 1, 0) - pltpu.roll(field, FRAME - 1, 0) - left - right
    operated = cnd[:, 128 : 128 + COLS] * lap
    res[:, 128 : 128 + COLS] = src[...] - (field + time_step * operated - prv[...])
    zero = jnp.zeros((FRAME, 128), jnp.float32)
    for ref in (res, cnd):
        ref[:, :128] = zero
        ref[:, 128 + COLS :] = zero

    def send_tile(t, jj):
        peer = 16 * t + jj
        src_ref = out.at[pl.ds(pl.multiple_of(8 * peer, 8), DEPTH)]
        dst_ref = inc.at[pl.ds(pl.multiple_of(8 * me, 8), DEPTH)]

        @pl.when(peer != me)
        def _():
            pltpu.make_async_remote_copy(
                src_ref, dst_ref, sems.at[0], sems.at[1], device_id={"tm": peer}, device_id_type=MESH
            ).start()

        @pl.when(peer == me)
        def _():
            pltpu.make_async_copy(src_ref, dst_ref, local_sem).start()

    @pl.loop(0, 8)
    def _(i):
        half = (i + 1) // 2
        t = (y + 4 + jnp.where(i % 2 == 0, half, -half) + 8) % 8
        strips = []
        for g in range(GROUPS):
            rows = pl.ds(TOP + DEPTH * g, 8)
            strips.append(
                [res[rows, pl.ds(pl.multiple_of(128 * t + 128 * d, 128), 128)] for d in range(3)]
            )
        for jj in range(16):
            message = jnp.zeros((8, 128), jnp.float32)
            for g in range(GROUPS):
                before, strip, after = strips[g]
                if jj == 0:
                    strip = jnp.where(lane >= 64, before, strip)
                if jj == 15:
                    strip = jnp.where(lane < 64, after, strip)
                piece = pltpu.roll(strip, (SPAN * g - TILE * jj + HALO) % 128, 1)
                message = jnp.where((lane >= SPAN * g) & (lane < SPAN * (g + 1)), piece, message)
            out[pl.ds(pl.multiple_of(128 * t + 8 * jj, 8), 8)] = message
        for jj in range(16):
            send_tile(t, jj)


def own_conductivity(me, y, cnd):
    lane = lax.broadcasted_iota(jnp.int32, (8, 128), 1)
    jj = me % 16
    packed = jnp.zeros((8, 128), jnp.float32)
    for g in range(GROUPS):
        rows = pl.ds(TOP + DEPTH * g, 8)
        before, strip, after = [
            cnd[rows, pl.ds(pl.multiple_of(128 * y + 128 * d, 128), 128)] for d in range(3)
        ]
        strip = jnp.where((jj == 0) & (lane >= 64), before, strip)
        strip = jnp.where((jj == 15) & (lane < 64), after, strip)
        amount = (SPAN * g - TILE * jj + HALO + 128) % 128
        piece = pltpu.roll(strip, amount, 1)
        packed = jnp.where((lane >= SPAN * g) & (lane < SPAN * (g + 1)), piece, packed)
    return packed


def split(value):
    high = value.astype(jnp.bfloat16)
    return high, (value - high.astype(jnp.float32)).astype(jnp.bfloat16)


def dot(a, b):
    return jnp.dot(a, b, preferred_element_type=jnp.float32)


def transform(matrices, offset, high, low):
    table_high = matrices[offset : offset + 128]
    table_low = matrices[offset + 128 : offset + 256]
    return dot(table_high, high) + (dot(table_high, low) + dot(table_low, high))


def solve(packed, inc, spec, shifts, matrices, select, out):
    points = jnp.concatenate(
        [inc[pl.ds(s, STEPS, stride=8), :] for s in range(DEPTH)], axis=1
    )
    spec[...] = transform(matrices, 0, *split(points))
    diffusion = [
        jnp.broadcast_to(time_step * packed[s : s + 1, :], (8, 128)) for s in range(DEPTH)
    ]
    weights = sweep_weights(SWEEPS)

    @pl.loop(0, 8)
    def _(i):
        real = pl.ds(pl.multiple_of(8 * i, 8), 8)
        imag = pl.ds(pl.multiple_of(8 * i + 64, 8), 8)
        couple = pl.ds(pl.multiple_of(8 * i + 128, 8), 8)
        one, two, b = shifts[real, :], shifts[imag, :], shifts[couple, :]
        cr, ci, g1, g2, gb = [], [], [], [], []
        for s in range(DEPTH):
            d = diffusion[s]
            p1, p2 = one + 4.0 * d, two + 4.0 * d
            inv = 1.0 / (p1 * p2 + b * b)
            q1, q2, qb = p2 * inv, p1 * inv, b * inv
            lanes = pl.ds(128 * s, 128)
            sr, si = spec[real, lanes], spec[imag, lanes]
            cr.append(q1 * sr + qb * si)
            ci.append(q2 * si - qb * sr)
            g1.append(q1 * d)
            g2.append(q2 * d)
            gb.append(qb * d)
        re = [weights[0] * v for v in cr]
        im = [weights[0] * v for v in ci]

        def neighbours(f):
            above = [pltpu.roll(f[DEPTH - 1], SPAN, 1)] + f[:-1]
            below = f[1:] + [pltpu.roll(f[0], 128 - SPAN, 1)]
            return [
                (above[s] + below[s]) + (pltpu.roll(f[s], 1, 1) + pltpu.roll(f[s], 127, 1))
                for s in range(DEPTH)
            ]

        for w in weights[1:]:
            nr, ni = neighbours(re), neighbours(im)
            re, im = (
                [
                    (1.0 - w) * re[s] + w * (cr[s] + g1[s] * nr[s] + gb[s] * ni[s])
                    for s in range(DEPTH)
                ],
                [
                    (1.0 - w) * im[s] + w * (ci[s] + g2[s] * ni[s] - gb[s] * nr[s])
                    for s in range(DEPTH)
                ],
            )
        for s in range(DEPTH):
            lanes = pl.ds(128 * s, 128)
            spec[real, lanes] = re[s]
            spec[imag, lanes] = im[s]

    high, low = split(spec[...])
    picked_high = dot(high, select[...]).astype(jnp.bfloat16)
    picked_low = dot(low, select[...]).astype(jnp.bfloat16)
    back = transform(matrices, 256, picked_high, picked_low)
    out[pl.ds(0, STEPS, stride=8), :] = back[:, :128]
    out[pl.ds(1, STEPS, stride=8), :] = back[:, 128:]


def main_kernel(
    src_in, it_in, ini_in, cnd_in, shifts_in, matrices_in, select_in,
    back_ref,
    it, src, prv, cnd, res, out, inc, spec, out2, shifts, matrices, select,
    send_sem, recv_sem, local_sem, table_sem, a2a_sem, a2a2_sem, self_sem,
):
    me = lax.axis_index("tm")
    slab = lax.axis_index("rows")
    y = me // 16
    after, before = (me + 1) % STEPS, (me + STEPS - 1) % STEPS
    down, up = (slab + 1) % 4, (slab + 3) % 4

    tables_in = [
        pltpu.make_async_copy(a, b, table_sem.at[i])
        for i, (a, b) in enumerate(
            [(shifts_in, shifts), (matrices_in, matrices), (select_in, select)]
        )
    ]
    inside = pl.ds(128, COLS)
    own = [
        pltpu.make_async_copy(it_in.at[0], it.at[pl.ds(8, ROWS)], local_sem.at[0]),
        pltpu.make_async_copy(src_in.at[0], src.at[pl.ds(8, ROWS)], local_sem.at[1]),
        pltpu.make_async_copy(cnd_in, cnd.at[pl.ds(8, ROWS), inside], local_sem.at[2]),
    ]
    for copy in own + tables_in:
        copy.start()

    barrier = pltpu.get_barrier_semaphore()
    for i in range(1, STEPS):
        pl.semaphore_signal(
            barrier, inc=1, device_id={"tm": (me + i) % STEPS}, device_id_type=MESH
        )
    greeted = [{"rows": down}, {"rows": up}]
    greeted += [{"tm": t, "rows": r} for t in (after, before) for r in (down, up)]
    for peer in greeted:
        pl.semaphore_signal(barrier, inc=1, device_id=peer, device_id_type=MESH)
    pl.semaphore_wait(barrier, STEPS - 1 + len(greeted))

    def remote(i, a, b, peer):
        return pltpu.make_async_remote_copy(
            a, b, send_sem.at[i], recv_sem.at[i], device_id=peer, device_id_type=MESH
        )

    def rows(ref, first, count):
        return ref.at[pl.ds(first, count)]

    it_own, src_own = it_in.at[0], src_in.at[0]

    def previous(value):
        return [
            remote(0, value, rows(prv, 8, ROWS), {"tm": after}),
            remote(1, rows(value, ROWS - HALO, HALO), rows(prv, TOP, HALO), {"tm": after, "rows": down}),
            remote(2, rows(value, 0, HALO), rows(prv, 8 + ROWS, HALO), {"tm": after, "rows": up}),
        ]

    @pl.when(me < STEPS - 1)
    def _():
        for copy in previous(it_own):
            copy.start()

    @pl.when(me == STEPS - 1)
    def _():
        for copy in previous(ini_in):
            copy.start()

    halos = [
        remote(3, rows(it_own, ROWS - HALO - 1, HALO + 1), rows(it, TOP - 1, HALO + 1), {"rows": down}),
        remote(4, rows(it_own, 0, HALO + 1), rows(it, 8 + ROWS, HALO + 1), {"rows": up}),
        remote(5, rows(src_own, ROWS - HALO, HALO), rows(src, TOP, HALO), {"rows": down}),
        remote(6, rows(src_own, 0, HALO), rows(src, 8 + ROWS, HALO), {"rows": up}),
        remote(7, rows(cnd_in, ROWS - HALO, HALO), cnd.at[pl.ds(TOP, HALO), inside], {"rows": down}),
        remote(8, rows(cnd_in, 0, HALO), cnd.at[pl.ds(8 + ROWS, HALO), inside], {"rows": up}),
    ]
    for copy in halos:
        copy.start()
    for copy in own:
        copy.wait()
    for copy in previous(ini_in) + halos:
        copy.wait()

    @pl.when(slab == 0)
    def _():
        for ref in (it, src, prv, cnd):
            ref[0:8, :] = jnp.zeros((8, ref.shape[1]), jnp.float32)

    @pl.when(slab == 3)
    def _():
        for ref in (it, src, prv, cnd):
            ref[8 + ROWS :, :] = jnp.zeros((8, ref.shape[1]), jnp.float32)

    residual_pack_send(me, y, slab, it, src, prv, cnd, res, out, inc, a2a_sem, self_sem.at[0])
    packed = own_conductivity(me, y, cnd)

    def wait_all(a, b, depth, sems, sem):
        share = (STEPS - 1) * depth
        pltpu.make_async_copy(rows(a, 0, depth), rows(b, 0, depth), sem).wait()
        pltpu.make_async_remote_copy(
            rows(a, 0, share), rows(b, 0, share), sems.at[0], sems.at[1],
            device_id={"tm": after}, device_id_type=MESH,
        ).wait()

    for copy in tables_in:
        copy.wait()
    wait_all(out, inc, DEPTH, a2a_sem, self_sem.at[0])
    solve(packed, inc, spec, shifts, matrices, select, out2)

    mine = pl.ds(pl.multiple_of(8 * me, 8), 2)
    pltpu.make_async_copy(out2.at[mine], back_ref.at[mine], self_sem.at[1]).start()

    @pl.loop(1, STEPS)
    def _(i):
        peer = (me + i) % STEPS
        pltpu.make_async_remote_copy(
            out2.at[pl.ds(pl.multiple_of(8 * peer, 8), 2)], back_ref.at[mine],
            a2a2_sem.at[0], a2a2_sem.at[1], device_id={"tm": peer}, device_id_type=MESH,
        ).start()

    wait_all(out2, back_ref, 2, a2a2_sem, self_sem.at[1])


def unpack_kernel(back, out):
    block = lax.broadcasted_iota(jnp.int32, (128, 128), 1) // 8
    tile = lax.broadcasted_iota(jnp.int32, (128, 128), 0)
    for h in range(2):
        x = back[pl.ds(h, 128, stride=8), :]
        for bit in (1, 2, 4, 8):
            lane_set, tile_set = (block & bit) != 0, (tile & bit) != 0
            from_next = pltpu.roll(pltpu.roll(x, 128 - bit, 0), 8 * bit, 1)
            from_last = pltpu.roll(pltpu.roll(x, bit, 0), 128 - 8 * bit, 1)
            moved = jnp.where(lane_set, from_next, from_last)
            x = jnp.where(lane_set == tile_set, x, moved)
        for t in range(8):
            out[0, 16 * h : 16 * h + 16, 128 * t : 128 * t + 128] = x[16 * t : 16 * t + 16]


def shards(source_term, iterate, initial, conductivity):
    shifts, matrices, select = tables()
    f32 = jnp.float32
    dma = pltpu.SemaphoreType.DMA
    back = pl.pallas_call(
        main_kernel,
        out_shape=jax.ShapeDtypeStruct((1024, 128), f32),
        in_specs=[pl.BlockSpec(memory_space=pl.ANY)] * 7,
        out_specs=pl.BlockSpec(memory_space=pl.ANY),
        scratch_shapes=[
            pltpu.VMEM((FRAME, COLS), f32),
            pltpu.VMEM((FRAME, COLS), f32),
            pltpu.VMEM((FRAME, COLS), f32),
            pltpu.VMEM((FRAME, COLS + 256), f32),
            pltpu.VMEM((FRAME, COLS + 256), f32),
            pltpu.VMEM((1024, 128), f32),
            pltpu.VMEM((1024, 128), f32),
            pltpu.VMEM((128, DEPTH * 128), f32),
            pltpu.VMEM((1024, 128), f32),
            pltpu.VMEM(shifts.shape, f32),
            pltpu.VMEM(matrices.shape, jnp.bfloat16),
            pltpu.VMEM(select.shape, jnp.bfloat16),
            dma((9,)), dma((9,)), dma((3,)), dma((3,)), dma((2,)), dma((2,)), dma((2,)),
        ],
        compiler_params=pltpu.CompilerParams(collective_id=0, has_side_effects=True),
        name="main",
    )(source_term, iterate, initial, conductivity, shifts, matrices, select)
    return pl.pallas_call(
        unpack_kernel,
        out_shape=jax.ShapeDtypeStruct((1, ROWS, COLS), f32),
        in_specs=[pl.BlockSpec(memory_space=pltpu.VMEM)],
        out_specs=pl.BlockSpec(memory_space=pltpu.VMEM),
        name="unpack",
    )(back)


def solution(mesh):
    in_specs = (P("tm", "rows", None), P("tm", "rows", None), P("rows", None), P("rows", None))
    out_specs = P("tm", "rows", None)
    return jax.shard_map(shards, mesh=mesh, in_specs=in_specs, out_specs=out_specs, check_vma=False)
```

time: 169 us -> 51.4 us (0.30)
  starting transfers between devices: 68 us -> 0 us
  waiting for transfers between devices: 53.5 us -> 0 us
  Pallas kernels: 0 us -> 51.3 us
  blocking collectives: 18.9 us -> 0 us
  other arithmetic: 18.5 us -> 0 us
  local copies, waits for them, and re-layouts: 6.82 us -> 0 us
  between operations: 1.86 us -> 0.01 us
    pallas_call x0 -> x2, Pallas kernels: none -> 51.3 us  [the longest x1 49.1 us: shards(): pl.pallas_call(main_kernel, out_shape=jax.ShapeDtypeStruct((1024, 128), f...]
    all_to_all x3 -> x0, waiting for transfers between devices: 37.7 us -> none  [the longest x1 14 us: shards(): lax.all_to_all(solved.reshape(2, 1, 2, window, half_block), 'tm', split_a...]
    all_to_all x3 -> x0, starting transfers between devices: 36.3 us -> none  [the longest x1 16.4 us: shards(): lax.all_to_all(residual.reshape(2, window, half_block), 'tm', split_axis=...]
    ppermute x13 -> x0, starting transfers between devices: 31.7 us -> none  [the longest x6 18.6 us: extended(): before = lax.ppermute(last, axis, up)]
    all_to_all x1 -> x0, blocking collectives: 18.9 us -> none  [shards(): lax.all_to_all(grid_points, 'tm', split_axis=0, concat_axis=2, tiled=True)]
    ppermute x13 -> x0, waiting for transfers between devices: 15.8 us -> none  [the longest x6 15 us: extended(): after = lax.ppermute(first, axis, down)]
    div x12 -> x0, other arithmetic: 14.9 us -> none  [the longest x6 8.21 us: relax(): (diag_two * defect_real + coupling * defect_imag) / determinant]
  transfers between devices with their start and end apart: 16 -> 0, of which waited for: 9 -> 0; matrix products, arithmetic and copies ran while one was open for 2% -> 0% of each run, Pallas kernels for 0% -> 0%
where the time goes in v1:
time: 51.4 us; the launch traced here: 51.3 us
  Pallas kernels  51.3 us (100%)
    pallas_call x1, Pallas kernels, shards(): pl.pallas_call(main_kernel, out_shape=jax.ShapeDtypeStruct((1024, 128), f...  49.1 us
    pallas_call x1, Pallas kernels, shards(): pl.pallas_call(unpack_kernel, out_shape=jax.ShapeDtypeStruct((1, ROWS, CO...  2.19 us

profile of v1, /device:TPU:1, one launch (start us, length us, event | category | flops | bytes accessed | tf_op | source)
XLA Modules:
  0.0 51.3 jit_solution(12820690704959923345)
XLA Ops:
  0.0 49.1 %main.1.back = f32[1024,128]{1,0:T(8,128)} custom-call(f32[1,32,1024]{2,1,0:T(8,128)} %src_in.1, f32[1,32,1024]{2,1,0:T(8,128)} %it_in.1, f32[32,1024]{1,0:T(8,128)} %ini_in.1, f32[32,1024]{1,0:T(8,128)} %cnd_in.1, f32[192,128]{1,0:T(8,128)} %constant.6.clone.shifts_in, bf16[512,128]{1,0:T(8,128)(2,1)} %constant.7.clone.matrices_in, ...), custom_call_target="tpu_custom_call" | custom-call | tf_op jit(solution)/shard_map/main/pallas_call | solution.py:367
  49.1 2.2 %unpack.1 = f32[1,32,1024]{2,1,0:T(8,128)} custom-call(f32[1024,128]{1,0:T(8,128)} %main.1.back), custom_call_target="tpu_custom_call" | custom-call | tf_op jit(solution)/shard_map/unpack/pallas_call | solution.py:390

commit v2 on v1

--- a/solution.py
+++ b/solution.py
@@ -21,6 +21,14 @@
 ROWS = 32
 TILE = 8
 HALO = SWEEPS - 1
+COLLECT_LOW = 16 * 5 + 2 * 2
+COLLECT_ALL = 16 * 5 + 2 * 5
+BLOCK = 32
+FAR_ROWS = (4, 3, 5, 2, 6, 1, 7, 0)
+FAR_FIRST = sorted(
+    [(dy, dz, dc) for dy in range(8) for dz in range(8) for dc in range(2) if dy or dz or dc],
+    key=lambda d: -min(d[0], 8 - d[0]) - min(d[1], 8 - d[1]),
+)
 SPAN = TILE + 2 * HALO
 GROUPS = 7
 DEPTH = 6
@@ -74,7 +82,7 @@
     return shifts, matrices, select.astype(jnp.bfloat16)
 
 
-def residual_pack_send(me, y, row_slab, it, src, prv, cnd, res, out, inc, sems, local_sem):
+def residual_pack_send(me, y, z, core, it, src, prv, cnd, res, out, inc, sems, local_sem, ready):
     lane = lax.broadcasted_iota(jnp.int32, (8, 128), 1)
     column = lax.broadcasted_iota(jnp.int32, (FRAME, COLS), 1)
     field = it[...]
@@ -88,44 +96,68 @@
         ref[:, :128] = zero
         ref[:, 128 + COLS :] = zero
 
-    def send_tile(t, jj):
-        peer = 16 * t + jj
-        src_ref = out.at[pl.ds(pl.multiple_of(8 * peer, 8), DEPTH)]
-        dst_ref = inc.at[pl.ds(pl.multiple_of(8 * me, 8), DEPTH)]
-
-        @pl.when(peer != me)
-        def _():
-            pltpu.make_async_remote_copy(
-                src_ref, dst_ref, sems.at[0], sems.at[1], device_id={"tm": peer}, device_id_type=MESH
-            ).start()
-
-        @pl.when(peer == me)
-        def _():
-            pltpu.make_async_copy(src_ref, dst_ref, local_sem).start()
+    def send(peer):
+        pltpu.make_async_remote_copy(
+            out.at[pl.ds(pl.multiple_of(8 * peer, 8), DEPTH)],
+            inc.at[pl.ds(pl.multiple_of(8 * me, 8), DEPTH)],
+            sems.at[0], sems.at[1], device_id={"tm": peer}, device_id_type=MESH,
+        ).start()
+
+    pl.semaphore_wait(ready.at[z // 4], 1)
+    low = z < 4
 
     @pl.loop(0, 8)
     def _(i):
         half = (i + 1) // 2
         t = (y + 4 + jnp.where(i % 2 == 0, half, -half) + 8) % 8
-        strips = []
+        plain, first, last = [], [], []
         for g in range(GROUPS):
             rows = pl.ds(TOP + DEPTH * g, 8)
-            strips.append(
-                [res[rows, pl.ds(pl.multiple_of(128 * t + 128 * d, 128), 128)] for d in range(3)]
+            before, strip, after = [
+                res[rows, pl.ds(pl.multiple_of(128 * t + 128 * d, 128), 128)] for d in range(3)
+            ]
+            amount = SPAN * g + HALO
+            plain.append(pltpu.roll(strip, amount, 1))
+            first.append(pltpu.roll(jnp.where(lane >= 64, before, strip), amount, 1))
+            last.append(pltpu.roll(jnp.where(lane < 64, after, strip), amount, 1))
+        for jj in range(16):
+            strips = first if jj == 0 else last if jj == 15 else plain
+            place = (lane + (128 - TILE * jj)) % 128
+            message = strips[0]
+            for g in range(1, GROUPS):
+                message = jnp.where(place >= SPAN * g, strips[g], message)
+            out[pl.ds(pl.multiple_of(128 * t + 8 * jj, 8), 8)] = pltpu.roll(
+                message, (128 - TILE * jj) % 128, 1
             )
-        for jj in range(16):
-            message = jnp.zeros((8, 128), jnp.float32)
-            for g in range(GROUPS):
-                before, strip, after = strips[g]
-                if jj == 0:
-                    strip = jnp.where(lane >= 64, before, strip)
-                if jj == 15:
-                    strip = jnp.where(lane < 64, after, strip)
-                piece = pltpu.roll(strip, (SPAN * g - TILE * jj + HALO) % 128, 1)
-                message = jnp.where((lane >= SPAN * g) & (lane < SPAN * (g + 1)), piece, message)
-            out[pl.ds(pl.multiple_of(128 * t + 8 * jj, 8), 8)] = message
-        for jj in range(16):
-            send_tile(t, jj)
+        for turn in range(1, 4):
+            for c in range(2):
+                send(16 * t + 2 * (z // 4 * 4 + (z + turn) % 4) + c)
+        send(16 * t + 2 * z + 1 - core)
+
+        @pl.when(t != y)
+        def _():
+            send(16 * t + 2 * z + core)
+
+        @pl.when(jnp.logical_not(low))
+        def _():
+            for plane in range(4):
+                for c in range(2):
+                    send(16 * t + 2 * plane + c)
+
+    mine = pl.ds(pl.multiple_of(8 * me, 8), DEPTH)
+    pltpu.make_async_copy(out.at[mine], inc.at[mine], local_sem).start()
+
+    @pl.when(low)
+    def _():
+        pl.semaphore_wait(ready.at[1], 1)
+
+        @pl.loop(0, 8)
+        def _(i):
+            half = (i + 1) // 2
+            t = (y + 4 + jnp.where(i % 2 == 0, half, -half) + 8) % 8
+            for plane in range(4, 8):
+                for c in range(2):
+                    send(16 * t + 2 * plane + c)
 
 
 def own_conductivity(me, y, cnd):
@@ -166,15 +198,15 @@
     )
     spec[...] = transform(matrices, 0, *split(points))
     diffusion = [
-        jnp.broadcast_to(time_step * packed[s : s + 1, :], (8, 128)) for s in range(DEPTH)
+        jnp.broadcast_to(time_step * packed[s : s + 1, :], (BLOCK, 128)) for s in range(DEPTH)
     ]
     weights = sweep_weights(SWEEPS)
 
-    @pl.loop(0, 8)
+    @pl.loop(0, 64 // BLOCK)
     def _(i):
-        real = pl.ds(pl.multiple_of(8 * i, 8), 8)
-        imag = pl.ds(pl.multiple_of(8 * i + 64, 8), 8)
-        couple = pl.ds(pl.multiple_of(8 * i + 128, 8), 8)
+        real = pl.ds(pl.multiple_of(BLOCK * i, BLOCK), BLOCK)
+        imag = pl.ds(pl.multiple_of(BLOCK * i + 64, BLOCK), BLOCK)
+        couple = pl.ds(pl.multiple_of(BLOCK * i + 128, BLOCK), BLOCK)
         one, two, b = shifts[real, :], shifts[imag, :], shifts[couple, :]
         cr, ci, g1, g2, gb = [], [], [], [], []
         for s in range(DEPTH):
@@ -229,11 +261,11 @@
     src_in, it_in, ini_in, cnd_in, shifts_in, matrices_in, select_in,
     back_ref,
     it, src, prv, cnd, res, out, inc, spec, out2, shifts, matrices, select,
-    send_sem, recv_sem, local_sem, table_sem, a2a_sem, a2a2_sem, self_sem,
+    send_sem, recv_sem, local_sem, table_sem, a2a_sem, a2a2_sem, self_sem, ready,
 ):
     me = lax.axis_index("tm")
     slab = lax.axis_index("rows")
-    y = me // 16
+    y, z, core = me // 16, me // 2 % 8, me % 2
     after, before = (me + 1) % STEPS, (me + STEPS - 1) % STEPS
     down, up = (slab + 1) % 4, (slab + 3) % 4
 
@@ -253,15 +285,40 @@
         copy.start()
 
     barrier = pltpu.get_barrier_semaphore()
-    for i in range(1, STEPS):
-        pl.semaphore_signal(
-            barrier, inc=1, device_id={"tm": (me + i) % STEPS}, device_id_type=MESH
-        )
-    greeted = [{"rows": down}, {"rows": up}]
+
+    def tell(sem, peer):
+        pl.semaphore_signal(sem, inc=1, device_id=peer, device_id_type=MESH)
+
+    greeted = [{"tm": after}, {"tm": before}, {"rows": down}, {"rows": up}]
     greeted += [{"tm": t, "rows": r} for t in (after, before) for r in (down, up)]
     for peer in greeted:
-        pl.semaphore_signal(barrier, inc=1, device_id=peer, device_id_type=MESH)
-    pl.semaphore_wait(barrier, STEPS - 1 + len(greeted))
+        tell(barrier, peer)
+    low = z < 4
+    for c in range(2):
+        for collector, when in ((COLLECT_LOW + c, low), (COLLECT_ALL + c, True)):
+
+            @pl.when(jnp.logical_and(me != collector, when))
+            def _():
+                tell(barrier, {"tm": collector})
+
+    collects_low, collects_all = me // 2 == COLLECT_LOW // 2, me // 2 == COLLECT_ALL // 2
+    heard = jnp.where(collects_low, STEPS // 2 - 1, 0) + jnp.where(collects_all, STEPS - 1, 0)
+    pl.semaphore_wait(barrier, len(greeted) + heard)
+
+    @pl.when(collects_low)
+    def _():
+        for dy in range(8):
+            for plane in range(4):
+                if 16 * dy + 2 * plane != COLLECT_LOW:
+                    tell(ready.at[0], {"tm": 16 * dy + 2 * plane + core})
+        pl.semaphore_signal(ready.at[0], inc=1)
+
+    @pl.when(collects_all)
+    def _():
+        for dy, dz, dc in FAR_FIRST:
+            if dc == 0:
+                tell(ready.at[1], {"tm": (y + dy) % 8 * 16 + (z + dz) % 8 * 2 + core})
+        pl.semaphore_signal(ready.at[1], inc=1)
 
     def remote(i, a, b, peer):
         return pltpu.make_async_remote_copy(
@@ -315,7 +372,7 @@
         for ref in (it, src, prv, cnd):
             ref[8 + ROWS :, :] = jnp.zeros((8, ref.shape[1]), jnp.float32)
 
-    residual_pack_send(me, y, slab, it, src, prv, cnd, res, out, inc, a2a_sem, self_sem.at[0])
+    residual_pack_send(me, y, z, core, it, src, prv, cnd, res, out, inc, a2a_sem, self_sem.at[0], ready)
     packed = own_conductivity(me, y, cnd)
 
     def wait_all(a, b, depth, sems, sem):
@@ -334,9 +391,8 @@
     mine = pl.ds(pl.multiple_of(8 * me, 8), 2)
     pltpu.make_async_copy(out2.at[mine], back_ref.at[mine], self_sem.at[1]).start()
 
-    @pl.loop(1, STEPS)
-    def _(i):
-        peer = (me + i) % STEPS
+    for dy, dz, dc in FAR_FIRST:
+        peer = (y + dy) % 8 * 16 + (z + dz) % 8 * 2 + (core + dc) % 2
         pltpu.make_async_remote_copy(
             out2.at[pl.ds(pl.multiple_of(8 * peer, 8), 2)], back_ref.at[mine],
             a2a2_sem.at[0], a2a2_sem.at[1], device_id={"tm": peer}, device_id_type=MESH,
@@ -383,6 +439,7 @@
             pltpu.VMEM(matrices.shape, jnp.bfloat16),
             pltpu.VMEM(select.shape, jnp.bfloat16),
             dma((9,)), dma((9,)), dma((3,)), dma((3,)), dma((2,)), dma((2,)), dma((2,)),
+            pltpu.SemaphoreType.REGULAR((2,)),
         ],
         compiler_params=pltpu.CompilerParams(collective_id=0, has_side_effects=True),
         name="main",

time: 51.4 us -> 44.3 us (0.86)
  Pallas kernels: 51.3 us -> 44.2 us
    pallas_call x1, Pallas kernels: 49.1 us -> 42 us  [shards(): pl.pallas_call(main_kernel, out_shape=jax.ShapeDtypeStruct((1024, 128), f...]
where the time goes in v2:
time: 44.3 us; the launch traced here: 44.2 us
  Pallas kernels  44.2 us (100%)
    pallas_call x1, Pallas kernels, shards(): pl.pallas_call(main_kernel, out_shape=jax.ShapeDtypeStruct((1024, 128), f...  42 us
    pallas_call x1, Pallas kernels, shards(): pl.pallas_call(unpack_kernel, out_shape=jax.ShapeDtypeStruct((1, ROWS, CO...  2.19 us

profile of v2, /device:TPU:1, one launch (start us, length us, event | category | flops | bytes accessed | tf_op | source)
XLA Modules:
  0.0 44.2 jit_solution(10928528681781713461)
XLA Ops:
  0.0 42.0 %main.1.back = f32[1024,128]{1,0:T(8,128)} custom-call(f32[1,32,1024]{2,1,0:T(8,128)} %src_in.1, f32[1,32,1024]{2,1,0:T(8,128)} %it_in.1, f32[32,1024]{1,0:T(8,128)} %ini_in.1, f32[32,1024]{1,0:T(8,128)} %cnd_in.1, f32[192,128]{1,0:T(8,128)} %constant.6.clone.shifts_in, bf16[512,128]{1,0:T(8,128)(2,1)} %constant.7.clone.matrices_in, ...), custom_call_target="tpu_custom_call" | custom-call | tf_op jit(solution)/shard_map/main/pallas_call | solution.py:423
  42.0 2.2 %unpack.1 = f32[1,32,1024]{2,1,0:T(8,128)} custom-call(f32[1024,128]{1,0:T(8,128)} %main.1.back), custom_call_target="tpu_custom_call" | custom-call | tf_op jit(solution)/shard_map/unpack/pallas_call | solution.py:447

commit v3 on v2

--- a/solution.py
+++ b/solution.py
@@ -23,7 +23,6 @@
 HALO = SWEEPS - 1
 COLLECT_LOW = 16 * 5 + 2 * 2
 COLLECT_ALL = 16 * 5 + 2 * 5
-BLOCK = 32
 FAR_ROWS = (4, 3, 5, 2, 6, 1, 7, 0)
 FAR_FIRST = sorted(
     [(dy, dz, dc) for dy in range(8) for dz in range(8) for dc in range(2) if dy or dz or dc],
@@ -192,62 +191,52 @@
     return dot(table_high, high) + (dot(table_high, low) + dot(table_low, high))
 
 
-def solve(packed, inc, spec, shifts, matrices, select, out):
+def solve(packed, inc, spec, coef, shifts, matrices, select, out):
     points = jnp.concatenate(
         [inc[pl.ds(s, STEPS, stride=8), :] for s in range(DEPTH)], axis=1
     )
     spec[...] = transform(matrices, 0, *split(points))
     diffusion = [
-        jnp.broadcast_to(time_step * packed[s : s + 1, :], (BLOCK, 128)) for s in range(DEPTH)
+        jnp.broadcast_to(time_step * packed[s : s + 1, :], (64, 128)) for s in range(DEPTH)
     ]
     weights = sweep_weights(SWEEPS)
 
-    @pl.loop(0, 64 // BLOCK)
-    def _(i):
-        real = pl.ds(pl.multiple_of(BLOCK * i, BLOCK), BLOCK)
-        imag = pl.ds(pl.multiple_of(BLOCK * i + 64, BLOCK), BLOCK)
-        couple = pl.ds(pl.multiple_of(BLOCK * i + 128, BLOCK), BLOCK)
-        one, two, b = shifts[real, :], shifts[imag, :], shifts[couple, :]
-        cr, ci, g1, g2, gb = [], [], [], [], []
+    half = STEPS // 2
+    real, imag = slice(0, half), slice(half, STEPS)
+    one, two, b = [shifts[half * i : half * (i + 1)] for i in range(3)]
+    for s in range(DEPTH):
+        d = diffusion[s]
+        p1, p2 = one + 4.0 * d, two + 4.0 * d
+        inv = 1.0 / (p1 * p2 + b * b)
+        q1, q2, qb = p2 * inv, p1 * inv, b * inv
+        lanes = slice(128 * s, 128 * s + 128)
+        sr, si = spec[real, lanes], spec[imag, lanes]
+        cr, ci = q1 * sr + qb * si, q2 * si - qb * sr
+        coef[0, real, lanes], coef[0, imag, lanes] = cr, ci
+        coef[1, real, lanes], coef[1, imag, lanes] = q1 * d, q2 * d
+        coef[2, real, lanes] = qb * d
+        spec[real, lanes], spec[imag, lanes] = weights[0] * cr, weights[0] * ci
+
+    row = lax.broadcasted_iota(jnp.int32, (256, 128), 0) % 128
+    column = lax.broadcasted_iota(jnp.int32, (256, 128), 1)
+    beside = jnp.where(jnp.abs(row - column) == 1, 1.0, 0.0).astype(jnp.bfloat16)
+
+    for w in weights[1:]:
+        fields = [spec[:, 128 * s : 128 * s + 128] for s in range(DEPTH)]
+        parts = jnp.concatenate([jnp.concatenate(split(f), axis=1) for f in fields], axis=0)
+        sides = dot(parts, beside)
+        top, bottom = pltpu.roll(fields[-1], SPAN, 1), pltpu.roll(fields[0], 128 - SPAN, 1)
         for s in range(DEPTH):
-            d = diffusion[s]
-            p1, p2 = one + 4.0 * d, two + 4.0 * d
-            inv = 1.0 / (p1 * p2 + b * b)
-            q1, q2, qb = p2 * inv, p1 * inv, b * inv
-            lanes = pl.ds(128 * s, 128)
-            sr, si = spec[real, lanes], spec[imag, lanes]
-            cr.append(q1 * sr + qb * si)
-            ci.append(q2 * si - qb * sr)
-            g1.append(q1 * d)
-            g2.append(q2 * d)
-            gb.append(qb * d)
-        re = [weights[0] * v for v in cr]
-        im = [weights[0] * v for v in ci]
-
-        def neighbours(f):
-            above = [pltpu.roll(f[DEPTH - 1], SPAN, 1)] + f[:-1]
-            below = f[1:] + [pltpu.roll(f[0], 128 - SPAN, 1)]
-            return [
-                (above[s] + below[s]) + (pltpu.roll(f[s], 1, 1) + pltpu.roll(f[s], 127, 1))
-                for s in range(DEPTH)
-            ]
-
-        for w in weights[1:]:
-            nr, ni = neighbours(re), neighbours(im)
-            re, im = (
-                [
-                    (1.0 - w) * re[s] + w * (cr[s] + g1[s] * nr[s] + gb[s] * ni[s])
-                    for s in range(DEPTH)
-                ],
-                [
-                    (1.0 - w) * im[s] + w * (ci[s] + g2[s] * ni[s] - gb[s] * nr[s])
-                    for s in range(DEPTH)
-                ],
-            )
-        for s in range(DEPTH):
-            lanes = pl.ds(128 * s, 128)
-            spec[real, lanes] = re[s]
-            spec[imag, lanes] = im[s]
+            above = fields[s - 1] if s else top
+            below = fields[s + 1] if s < DEPTH - 1 else bottom
+            near = (above + below) + sides[128 * s : 128 * s + 128]
+            nr, ni = near[:half], near[half:]
+            lanes = slice(128 * s, 128 * s + 128)
+            gb = coef[2, real, lanes]
+            nr2 = coef[0, real, lanes] + coef[1, real, lanes] * nr + gb * ni
+            ni2 = coef[0, imag, lanes] + coef[1, imag, lanes] * ni - gb * nr
+            spec[real, lanes] = (1.0 - w) * fields[s][:half] + w * nr2
+            spec[imag, lanes] = (1.0 - w) * fields[s][half:] + w * ni2
 
     high, low = split(spec[...])
     picked_high = dot(high, select[...]).astype(jnp.bfloat16)
@@ -260,7 +249,7 @@
 def main_kernel(
     src_in, it_in, ini_in, cnd_in, shifts_in, matrices_in, select_in,
     back_ref,
-    it, src, prv, cnd, res, out, inc, spec, out2, shifts, matrices, select,
+    it, src, prv, cnd, res, out, inc, spec, coef, out2, shifts, matrices, select,
     send_sem, recv_sem, local_sem, table_sem, a2a_sem, a2a2_sem, self_sem, ready,
 ):
     me = lax.axis_index("tm")
@@ -281,9 +270,6 @@
         pltpu.make_async_copy(src_in.at[0], src.at[pl.ds(8, ROWS)], local_sem.at[1]),
         pltpu.make_async_copy(cnd_in, cnd.at[pl.ds(8, ROWS), inside], local_sem.at[2]),
     ]
-    for copy in own + tables_in:
-        copy.start()
-
     barrier = pltpu.get_barrier_semaphore()
 
     def tell(sem, peer):
@@ -301,6 +287,8 @@
             def _():
                 tell(barrier, {"tm": collector})
 
+    for copy in own + tables_in:
+        copy.start()
     collects_low, collects_all = me // 2 == COLLECT_LOW // 2, me // 2 == COLLECT_ALL // 2
     heard = jnp.where(collects_low, STEPS // 2 - 1, 0) + jnp.where(collects_all, STEPS - 1, 0)
     pl.semaphore_wait(barrier, len(greeted) + heard)
@@ -386,7 +374,7 @@
     for copy in tables_in:
         copy.wait()
     wait_all(out, inc, DEPTH, a2a_sem, self_sem.at[0])
-    solve(packed, inc, spec, shifts, matrices, select, out2)
+    solve(packed, inc, spec, coef, shifts, matrices, select, out2)
 
     mine = pl.ds(pl.multiple_of(8 * me, 8), 2)
     pltpu.make_async_copy(out2.at[mine], back_ref.at[mine], self_sem.at[1]).start()
@@ -401,19 +389,25 @@
     wait_all(out2, back_ref, 2, a2a2_sem, self_sem.at[1])
 
 
-def unpack_kernel(back, out):
-    block = lax.broadcasted_iota(jnp.int32, (128, 128), 1) // 8
-    tile = lax.broadcasted_iota(jnp.int32, (128, 128), 0)
+def unpack_kernel(back, out, rows):
+    block = lax.broadcasted_iota(jnp.int32, (8, 128), 1) // 8
     for h in range(2):
-        x = back[pl.ds(h, 128, stride=8), :]
+        v = [back[pl.ds(8 * tile + h, 8, stride=128), :] for tile in range(16)]
         for bit in (1, 2, 4, 8):
-            lane_set, tile_set = (block & bit) != 0, (tile & bit) != 0
-            from_next = pltpu.roll(pltpu.roll(x, 128 - bit, 0), 8 * bit, 1)
-            from_last = pltpu.roll(pltpu.roll(x, bit, 0), 128 - 8 * bit, 1)
-            moved = jnp.where(lane_set, from_next, from_last)
-            x = jnp.where(lane_set == tile_set, x, moved)
-        for t in range(8):
-            out[0, 16 * h : 16 * h + 16, 128 * t : 128 * t + 128] = x[16 * t : 16 * t + 16]
+            there = (block & bit) != 0
+            for tile in range(16):
+                if not tile & bit:
+                    p, q = v[tile], v[tile + bit]
+                    v[tile] = jnp.where(there, pltpu.roll(q, 8 * bit, 1), p)
+                    v[tile + bit] = jnp.where(there, q, pltpu.roll(p, 128 - 8 * bit, 1))
+        for i in range(16):
+            row = 16 * h + i
+            rows[pl.ds(64 * (row // 8) + row % 8, 8, stride=8), :] = v[i]
+    for i in range(ROWS // 8):
+        for group in range(8):
+            out[0, 8 * i : 8 * i + 8, 128 * group : 128 * group + 128] = rows[
+                64 * i + 8 * group : 64 * i + 8 * group + 8
+            ]
 
 
 def shards(source_term, iterate, initial, conductivity):
@@ -434,6 +428,7 @@
             pltpu.VMEM((1024, 128), f32),
             pltpu.VMEM((1024, 128), f32),
             pltpu.VMEM((128, DEPTH * 128), f32),
+            pltpu.VMEM((3, 128, DEPTH * 128), f32),
             pltpu.VMEM((1024, 128), f32),
             pltpu.VMEM(shifts.shape, f32),
             pltpu.VMEM(matrices.shape, jnp.bfloat16),
@@ -449,6 +444,7 @@
         out_shape=jax.ShapeDtypeStruct((1, ROWS, COLS), f32),
         in_specs=[pl.BlockSpec(memory_space=pltpu.VMEM)],
         out_specs=pl.BlockSpec(memory_space=pltpu.VMEM),
+        scratch_shapes=[pltpu.VMEM((8 * ROWS, 128), f32)],
         name="unpack",
     )(back)
 

time: 44.3 us -> 43.4 us (0.980)
  Pallas kernels: 44.2 us -> 43.2 us
    pallas_call x1, Pallas kernels: 42 us -> 41.1 us  [shards(): pl.pallas_call(main_kernel, out_shape=jax.ShapeDtypeStruct((1024, 128), f...]
where the time goes in v3:
time: 43.4 us; the launch traced here: 43.2 us
  Pallas kernels  43.2 us (100%)
    pallas_call x1, Pallas kernels, shards(): pl.pallas_call(main_kernel, out_shape=jax.ShapeDtypeStruct((1024, 128), f...  41.1 us
    pallas_call x1, Pallas kernels, shards(): pl.pallas_call(unpack_kernel, out_shape=jax.ShapeDtypeStruct((1, ROWS, CO...  2.07 us

profile of v3, /device:TPU:1, one launch (start us, length us, event | category | flops | bytes accessed | tf_op | source)
XLA Modules:
  0.0 43.2 jit_solution(3934223148823014575)
XLA Ops:
  0.0 41.1 %main.1.back = f32[1024,128]{1,0:T(8,128)} custom-call(f32[1,32,1024]{2,1,0:T(8,128)} %src_in.1, f32[1,32,1024]{2,1,0:T(8,128)} %it_in.1, f32[32,1024]{1,0:T(8,128)} %ini_in.1, f32[32,1024]{1,0:T(8,128)} %cnd_in.1, f32[192,128]{1,0:T(8,128)} %constant.6.clone.shifts_in, bf16[512,128]{1,0:T(8,128)(2,1)} %constant.7.clone.matrices_in, ...), custom_call_target="tpu_custom_call" | custom-call | tf_op jit(solution)/shard_map/main/pallas_call | solution.py:417
  41.1 2.1 %unpack.1 = f32[1,32,1024]{2,1,0:T(8,128)} custom-call(f32[1024,128]{1,0:T(8,128)} %main.1.back), custom_call_target="tpu_custom_call" | custom-call | tf_op jit(solution)/shard_map/unpack/pallas_call | solution.py:442

commit v4 on v3

--- a/solution.py
+++ b/solution.py
@@ -191,30 +191,37 @@
     return dot(table_high, high) + (dot(table_high, low) + dot(table_low, high))
 
 
-def solve(packed, inc, spec, coef, shifts, matrices, select, out):
+def prepare(packed, coef, shifts):
+    half = STEPS // 2
+    real, imag = slice(0, half), slice(half, STEPS)
+    one, two, b = [shifts[half * i : half * (i + 1)] for i in range(3)]
+    for s in range(DEPTH):
+        d = jnp.broadcast_to(time_step * packed[s : s + 1, :], (half, 128))
+        p1, p2 = one + 4.0 * d, two + 4.0 * d
+        inv = 1.0 / (p1 * p2 + b * b)
+        q1, q2, qb = p2 * inv, p1 * inv, b * inv
+        lanes = slice(128 * s, 128 * s + 128)
+        coef[0, real, lanes], coef[0, imag, lanes] = q1, q2
+        coef[1, real, lanes], coef[1, imag, lanes] = q1 * d, q2 * d
+        coef[2, real, lanes], coef[2, imag, lanes] = qb * d, qb
+
+
+def solve(inc, spec, coef, matrices, select, out):
     points = jnp.concatenate(
         [inc[pl.ds(s, STEPS, stride=8), :] for s in range(DEPTH)], axis=1
     )
     spec[...] = transform(matrices, 0, *split(points))
-    diffusion = [
-        jnp.broadcast_to(time_step * packed[s : s + 1, :], (64, 128)) for s in range(DEPTH)
-    ]
     weights = sweep_weights(SWEEPS)
 
     half = STEPS // 2
     real, imag = slice(0, half), slice(half, STEPS)
-    one, two, b = [shifts[half * i : half * (i + 1)] for i in range(3)]
     for s in range(DEPTH):
-        d = diffusion[s]
-        p1, p2 = one + 4.0 * d, two + 4.0 * d
-        inv = 1.0 / (p1 * p2 + b * b)
-        q1, q2, qb = p2 * inv, p1 * inv, b * inv
         lanes = slice(128 * s, 128 * s + 128)
         sr, si = spec[real, lanes], spec[imag, lanes]
-        cr, ci = q1 * sr + qb * si, q2 * si - qb * sr
+        qb = coef[2, imag, lanes]
+        cr = coef[0, real, lanes] * sr + qb * si
+        ci = coef[0, imag, lanes] * si - qb * sr
         coef[0, real, lanes], coef[0, imag, lanes] = cr, ci
-        coef[1, real, lanes], coef[1, imag, lanes] = q1 * d, q2 * d
-        coef[2, real, lanes] = qb * d
         spec[real, lanes], spec[imag, lanes] = weights[0] * cr, weights[0] * ci
 
     row = lax.broadcasted_iota(jnp.int32, (256, 128), 0) % 128
@@ -293,21 +300,6 @@
     heard = jnp.where(collects_low, STEPS // 2 - 1, 0) + jnp.where(collects_all, STEPS - 1, 0)
     pl.semaphore_wait(barrier, len(greeted) + heard)
 
-    @pl.when(collects_low)
-    def _():
-        for dy in range(8):
-            for plane in range(4):
-                if 16 * dy + 2 * plane != COLLECT_LOW:
-                    tell(ready.at[0], {"tm": 16 * dy + 2 * plane + core})
-        pl.semaphore_signal(ready.at[0], inc=1)
-
-    @pl.when(collects_all)
-    def _():
-        for dy, dz, dc in FAR_FIRST:
-            if dc == 0:
-                tell(ready.at[1], {"tm": (y + dy) % 8 * 16 + (z + dz) % 8 * 2 + core})
-        pl.semaphore_signal(ready.at[1], inc=1)
-
     def remote(i, a, b, peer):
         return pltpu.make_async_remote_copy(
             a, b, send_sem.at[i], recv_sem.at[i], device_id=peer, device_id_type=MESH
@@ -345,6 +337,22 @@
     ]
     for copy in halos:
         copy.start()
+
+    @pl.when(collects_low)
+    def _():
+        for dy in range(8):
+            for plane in range(4):
+                if 16 * dy + 2 * plane != COLLECT_LOW:
+                    tell(ready.at[0], {"tm": 16 * dy + 2 * plane + core})
+        pl.semaphore_signal(ready.at[0], inc=1)
+
+    @pl.when(collects_all)
+    def _():
+        for dy, dz, dc in FAR_FIRST:
+            if dc == 0:
+                tell(ready.at[1], {"tm": (y + dy) % 8 * 16 + (z + dz) % 8 * 2 + core})
+        pl.semaphore_signal(ready.at[1], inc=1)
+
     for copy in own:
         copy.wait()
     for copy in previous(ini_in) + halos:
@@ -373,8 +381,9 @@
 
     for copy in tables_in:
         copy.wait()
+    prepare(packed, coef, shifts)
     wait_all(out, inc, DEPTH, a2a_sem, self_sem.at[0])
-    solve(packed, inc, spec, coef, shifts, matrices, select, out2)
+    solve(inc, spec, coef, matrices, select, out2)
 
     mine = pl.ds(pl.multiple_of(8 * me, 8), 2)
     pltpu.make_async_copy(out2.at[mine], back_ref.at[mine], self_sem.at[1]).start()

time: 43.4 us -> 43.3 us (level)
  no operation moved by 1% of the time
where the time goes in v4:
time: 43.3 us; the launch traced here: 43.2 us
  Pallas kernels  43.2 us (100%)
    pallas_call x1, Pallas kernels, shards(): pl.pallas_call(main_kernel, out_shape=jax.ShapeDtypeStruct((1024, 128), f...  41.1 us
    pallas_call x1, Pallas kernels, shards(): pl.pallas_call(unpack_kernel, out_shape=jax.ShapeDtypeStruct((1, ROWS, CO...  2.07 us

profile of v4, /device:TPU:1, one launch (start us, length us, event | category | flops | bytes accessed | tf_op | source)
XLA Modules:
  0.0 43.2 jit_solution(17374133940546435716)
XLA Ops:
  0.0 41.1 %main.1.back = f32[1024,128]{1,0:T(8,128)} custom-call(f32[1,32,1024]{2,1,0:T(8,128)} %src_in.1, f32[1,32,1024]{2,1,0:T(8,128)} %it_in.1, f32[32,1024]{1,0:T(8,128)} %ini_in.1, f32[32,1024]{1,0:T(8,128)} %cnd_in.1, f32[192,128]{1,0:T(8,128)} %constant.6.clone.shifts_in, bf16[512,128]{1,0:T(8,128)(2,1)} %constant.7.clone.matrices_in, ...), custom_call_target="tpu_custom_call" | custom-call | tf_op jit(solution)/shard_map/main/pallas_call | solution.py:426
  41.1 2.1 %unpack.1 = f32[1,32,1024]{2,1,0:T(8,128)} custom-call(f32[1024,128]{1,0:T(8,128)} %main.1.back), custom_call_target="tpu_custom_call" | custom-call | tf_op jit(solution)/shard_map/unpack/pallas_call | solution.py:451

commit v5 on v4

--- a/solution.py
+++ b/solution.py
@@ -152,8 +152,7 @@
 
         @pl.loop(0, 8)
         def _(i):
-            half = (i + 1) // 2
-            t = (y + 4 + jnp.where(i % 2 == 0, half, -half) + 8) % 8
+            t = (y + i) % 4 + jnp.where(i < 4, 4, 0)
             for plane in range(4, 8):
                 for c in range(2):
                     send(16 * t + 2 * plane + c)
@@ -300,6 +299,21 @@
     heard = jnp.where(collects_low, STEPS // 2 - 1, 0) + jnp.where(collects_all, STEPS - 1, 0)
     pl.semaphore_wait(barrier, len(greeted) + heard)
 
+    @pl.when(collects_low)
+    def _():
+        for dy in range(8):
+            for plane in range(4):
+                if 16 * dy + 2 * plane != COLLECT_LOW:
+                    tell(ready.at[0], {"tm": 16 * dy + 2 * plane + core})
+        pl.semaphore_signal(ready.at[0], inc=1)
+
+    @pl.when(collects_all)
+    def _():
+        for dy, dz, dc in FAR_FIRST:
+            if dc == 0:
+                tell(ready.at[1], {"tm": (y + dy) % 8 * 16 + (z + dz) % 8 * 2 + core})
+        pl.semaphore_signal(ready.at[1], inc=1)
+
     def remote(i, a, b, peer):
         return pltpu.make_async_remote_copy(
             a, b, send_sem.at[i], recv_sem.at[i], device_id=peer, device_id_type=MESH
@@ -337,22 +351,6 @@
     ]
     for copy in halos:
         copy.start()
-
-    @pl.when(collects_low)
-    def _():
-        for dy in range(8):
-            for plane in range(4):
-                if 16 * dy + 2 * plane != COLLECT_LOW:
-                    tell(ready.at[0], {"tm": 16 * dy + 2 * plane + core})
-        pl.semaphore_signal(ready.at[0], inc=1)
-
-    @pl.when(collects_all)
-    def _():
-        for dy, dz, dc in FAR_FIRST:
-            if dc == 0:
-                tell(ready.at[1], {"tm": (y + dy) % 8 * 16 + (z + dz) % 8 * 2 + core})
-        pl.semaphore_signal(ready.at[1], inc=1)
-
     for copy in own:
         copy.wait()
     for copy in previous(ini_in) + halos:

time: 43.3 us -> 43.3 us (level)
  no operation moved by 1% of the time
where the time goes in v5:
time: 43.3 us; the launch traced here: 43.2 us
  Pallas kernels  43.2 us (100%)
    pallas_call x1, Pallas kernels, shards(): pl.pallas_call(main_kernel, out_shape=jax.ShapeDtypeStruct((1024, 128), f...  41.1 us
    pallas_call x1, Pallas kernels, shards(): pl.pallas_call(unpack_kernel, out_shape=jax.ShapeDtypeStruct((1, ROWS, CO...  2.07 us

profile of v5, /device:TPU:1, one launch (start us, length us, event | category | flops | bytes accessed | tf_op | source)
XLA Modules:
  0.0 43.2 jit_solution(11902258489563446674)
XLA Ops:
  0.0 41.1 %main.1.back = f32[1024,128]{1,0:T(8,128)} custom-call(f32[1,32,1024]{2,1,0:T(8,128)} %src_in.1, f32[1,32,1024]{2,1,0:T(8,128)} %it_in.1, f32[32,1024]{1,0:T(8,128)} %ini_in.1, f32[32,1024]{1,0:T(8,128)} %cnd_in.1, f32[192,128]{1,0:T(8,128)} %constant.6.clone.shifts_in, bf16[512,128]{1,0:T(8,128)(2,1)} %constant.7.clone.matrices_in, ...), custom_call_target="tpu_custom_call" | custom-call | tf_op jit(solution)/shard_map/main/pallas_call | solution.py:424
  41.1 2.1 %unpack.1 = f32[1,32,1024]{2,1,0:T(8,128)} custom-call(f32[1024,128]{1,0:T(8,128)} %main.1.back), custom_call_target="tpu_custom_call" | custom-call | tf_op jit(solution)/shard_map/unpack/pallas_call | solution.py:449
